TPU v7x, 128 devices: a whole 4x4x4 slice. The times are simulated.
128 devices in a mesh: batch: 2 (over x_hi), blk: 64 (over x_lo, z, y, core).
Axes of the slice: x: 4 (x_hi: 2, x_lo: 2; x = x_hi * 2 + x_lo), y: 4, z: 4, core: 2. Of those that a mesh axis runs over, the one named last changes fastest.
Arguments:
- stream: bfloat16 [131072, 1024], P(('batch', 'blk')), parts along dimension 0, may hold values from -6 to 6
- norm_gain: float32 [4, 1024], replicated, may hold values from 0.1 to 1.9
- norm_bias: float32 [4, 1024], replicated, may hold values from -3 to 3
- proj_in: bfloat16 [4, 1024, 512], replicated, may hold values from -0.1875 to 0.1875
- convolution_taps: bfloat16 [4, 3, 512, 512], replicated, may hold values from -0.15625 to 0.15625
- output_projection: bfloat16 [4, 512, 1024], replicated, may hold values from -0.25 to 0.25
Outputs:
- result: bfloat16 [131072, 1024], P(('batch', 'blk')), parts along dimension 0
There are 2 independent parts, one for each index of `batch`. A program takes and returns all parts, laid end to end along the dimension named above; an argument that names none is the same for every part. Nothing has to cross between parts.
All inputs are finite; a program needn't handle non-finite values.
Results may differ from a plain program's by a relative error of at most 0.017.
Values may be sent and summed in bfloat16 or wider, within the bound.
A program may use at most 64 MiB of HBM per device.

v0:
```python
import jax
import jax.numpy as jnp
from jax import lax
from jax.sharding import PartitionSpec as P

LAYERS = 4
DILATION_START = 512


EPSILON = 1e-05


def passed_along(array, axis, by):
    peers = lax.axis_size(axis)
    return lax.ppermute(array, axis, [(i, (i + by) % peers) for i in range(peers)])


def extended(array, sides, width):
    for axis, dim in sides:
        peers, length = (lax.axis_size(axis), array.shape[dim])
        up = [(i, (i + 1) % peers) for i in range(peers)]
        down = [(j, i) for i, j in up]
        last = lax.slice_in_dim(array, length - width, length, axis=dim)
        leading = lax.slice_in_dim(array, 0, width, axis=dim)
        before = lax.ppermute(last, axis, up)
        after = lax.ppermute(leading, axis, down)
        array = jnp.concatenate([before, array, after], axis=dim)
    return array


def normalize(stream, scales, offsets):
    values = stream.astype(jnp.float32)
    average = jnp.mean(values, axis=1, keepdims=True)
    centred_values = values - average
    variance = jnp.mean(centred_values * centred_values, axis=1, keepdims=True)
    return (centred_values * lax.rsqrt(variance + EPSILON) * scales + offsets).astype(jnp.bfloat16)


def direct_move(block, offset):
    return passed_along(block, "blk", offset)


def gather_distant(narrow, distance):
    earlier = direct_move(narrow, distance)
    after = direct_move(narrow, -distance)
    return (earlier, after)


def body(stream, norm_gain, norm_bias, proj_in, convolution_taps, output_projection):
    shard_rows = stream.shape[0]
    for block_depth in range(LAYERS):
        dilation_factor = DILATION_START * 2**block_depth
        normed = normalize(stream, norm_gain[block_depth], norm_bias[block_depth])
        narrow = jnp.dot(normed, proj_in[block_depth], preferred_element_type=jnp.float32).astype(
            jnp.bfloat16
        )
        kernel = convolution_taps[block_depth]
        middle = jnp.dot(narrow, kernel[1], preferred_element_type=jnp.float32)
        if dilation_factor < shard_rows:
            padded = extended(narrow, (("blk", 0),), dilation_factor)
            convolved = middle + jnp.dot(
                padded[:shard_rows], kernel[0], preferred_element_type=jnp.float32
            )
            convolved = convolved + jnp.dot(
                padded[2 * dilation_factor :], kernel[2], preferred_element_type=jnp.float32
            )
        else:
            earlier, after = gather_distant(narrow, dilation_factor // shard_rows)
            convolved = middle + jnp.dot(earlier, kernel[0], preferred_element_type=jnp.float32)
            convolved = convolved + jnp.dot(after, kernel[2], preferred_element_type=jnp.float32)
        activated = jax.nn.gelu(convolved, approximate=False).astype(jnp.bfloat16)
        update = jnp.dot(
            activated, output_projection[block_depth], preferred_element_type=jnp.float32
        )
        stream = (stream.astype(jnp.float32) + update).astype(jnp.bfloat16)
    return stream


def solution(mesh):
    return jax.shard_map(
        body,
        mesh=mesh,
        in_specs=(P(("batch", "blk"), None), P(), P(), P(), P(), P()),
        out_specs=P(("batch", "blk"), None),
        check_vma=False,
    )
```

profile of v0, /device:TPU:16, one launch (start us, length us, event | category | flops | bytes accessed | tf_op | source)
XLA Modules:
  0.0 181.3 jit_solution(1730353968588859784)
XLA Ops:
  0.0 0.9 fusion.286
  0.9 0.9 fusion.287
  1.8 2.9 %copy.7 = bf16[1024,1024]{0,1:T(8,128)(2,1)S(1)} copy(bf16[1024,1024]{1,0:T(8,128)(2,1)} %param.6) | data formatting | bytes 4194304 | tf_op args[0]
  4.6 0.4 convert_reduce_fusion.3
  5.0 0.6 fusion.20
  5.6 2.7 %fusion.101 = bf16[1024,512]{1,0:T(8,128)(2,1)S(1)} fusion(bf16[1024,1024]{0,1:T(8,128)(2,1)S(1)} %copy.7, f32[1024]{0:T(1024)S(1)} %bitcast.101, f32[1024]{0:T(1024)S(1)} %bitcast.100, f32[1024]{0:T(1024)S(1)} %add_rsqrt_fusion.3, f32[1024]{0:T(1024)S(1)} %broadcast_multiply_fusion.3, bf16[4,1024,512]{2,1,0:T(8,128)(2,1)} %param.9), kind=kOutput, calls=%fused_computation.143 | convolution fusion | flops 1080557568 | bytes 4210688 | tf_op jit(solution)/shard_map/dot_general | solution.py:54
  8.3 0.1 fusion.285
  8.4 0.1 collective-permute-start
  8.5 1.7 collective-permute-start.1
  10.2 3.1 %fusion.144 = f32[1024,512]{1,0:T(8,128)} fusion(bf16[1024,512]{1,0:T(8,128)(2,1)S(1)} %fusion.101, bf16[4,3,512,512]{3,2,1,0:T(8,128)(2,1)} %param.10), kind=kOutput, calls=%fused_computation.182 | convolution fusion | flops 536870912 | bytes 3670016 | tf_op jit(solution)/shard_map/dot_general | solution.py:58
  13.3 3.8 %collective-permute-done = bf16[512,512]{1,0:T(8,128)(2,1)S(1)} collective-permute-done((bf16[512,512]{1,0:T(8,128)(2,1)S(1)}, bf16[512,512]{1,0:T(8,128)(2,1)S(1)}, u32[]{:S(2)}, u32[]{:S(2)}) %collective-permute-start) | collective-permute-done | bytes 524320 | tf_op jit(solution)/shard_map/ppermute | solution.py:25
  17.1 3.0 %fusion.105 = f32[1024,512]{1,0:T(8,128)} fusion(bf16[1024,512]{1,0:T(8,128)(2,1)S(1)} %fusion.101, bf16[512,512]{1,0:T(8,128)(2,1)S(1)} %collective-permute-done, bf16[4,3,512,512]{3,2,1,0:T(8,128)(2,1)} %param.10), kind=kOutput, calls=%fused_computation.147 | convolution fusion | flops 538968064 | bytes 4194304 | tf_op jit(solution)/shard_map/dot_general | solution.py:61
  20.1 0.0 collective-permute-done.1
  20.1 10.1 %convert_reduce_fusion.2 = (f32[1024]{0:T(1024)S(1)}, bf16[1024,1024]{0,1:T(8,128)(2,1)}) fusion(bf16[4,512,1024]{2,1,0:T(8,128)(2,1)} %param.11, f32[1024,512]{1,0:T(8,128)} %fusion.144, f32[1024,512]{1,0:T(8,128)} %fusion.105, bf16[512,512]{1,0:T(8,128)(2,1)} %collective-permute-done.1, bf16[1024,512]{1,0:T(8,128)(2,1)S(1)} %fusion.101, ...), kind=kOutput, calls=%fused_computation.8 | convolution fusion | flops 1653079040 | bytes 11538432 | tf_op jit(solution)/shard_map/dot_general | solution.py:72
  30.3 0.0 copy-start
  30.3 2.3 %fusion.16 = f32[1024]{0:T(1024)S(1)} fusion(bf16[1024,1024]{0,1:T(8,128)(2,1)} %get-tuple-element.16, f32[1024]{0:T(1024)S(1)} %broadcast_multiply_fusion.2), kind=kLoop, calls=%fused_computation.28 | loop fusion | flops 4193280 | bytes 2105344 | tf_op jit(solution)/shard_map/reduce_sum | solution.py:35
  32.6 0.0 copy-done
  32.6 2.8 %fusion.98 = bf16[1024,512]{1,0:T(8,128)(2,1)S(1)} fusion(bf16[1024,1024]{0,1:T(8,128)(2,1)S(1)} %copy-done, f32[1024]{0:T(1024)S(1)} %bitcast.99, f32[1024]{0:T(1024)S(1)} %bitcast.98, f32[1024]{0:T(1024)S(1)} %add_rsqrt_fusion.2, f32[1024]{0:T(1024)S(1)} %broadcast_multiply_fusion.2, bf16[4,1024,512]{2,1,0:T(8,128)(2,1)} %param.9), kind=kOutput, calls=%fused_computation.142 | convolution fusion | flops 1080557568 | bytes 4210688 | tf_op jit(solution)/shard_map/dot_general | solution.py:54
  35.5 0.1 collective-permute-start.2
  35.6 1.7 collective-permute-start.3
  37.3 1.7 fusion.139
  39.0 10.7 %collective-permute-done.2 = bf16[1024,512]{1,0:T(8,128)(2,1)S(1)} collective-permute-done((bf16[1024,512]{1,0:T(8,128)(2,1)S(1)}, bf16[1024,512]{1,0:T(8,128)(2,1)S(1)}, u32[]{:S(2)}, u32[]{:S(2)}) %collective-permute-start.2) | collective-permute-done | bytes 1048608 | tf_op jit(solution)/shard_map/ppermute | solution.py:15
  49.8 3.1 %fusion.137 = f32[1024,512]{1,0:T(8,128)} fusion(bf16[1024,512]{1,0:T(8,128)(2,1)S(1)} %collective-permute-done.2, bf16[4,3,512,512]{3,2,1,0:T(8,128)(2,1)} %param.10), kind=kOutput, calls=%fused_computation.176 | convolution fusion | flops 536870912 | bytes 3670016 | tf_op jit(solution)/shard_map/dot_general | solution.py:69
  52.8 0.0 collective-permute-done.3
  52.8 9.8 %convert_reduce_fusion.1 = (f32[1024]{0:T(1024)S(1)}, bf16[1024,1024]{0,1:T(8,128)(2,1)}) fusion(bf16[4,512,1024]{2,1,0:T(8,128)(2,1)} %param.11, f32[1024,512]{1,0:T(8,128)S(1)} %fusion.139, f32[1024,512]{1,0:T(8,128)} %fusion.137, bf16[1024,512]{1,0:T(8,128)(2,1)S(1)} %collective-permute-done.3, bf16[4,3,512,512]{3,2,1,0:T(8,128)(2,1)} %param.10, ...), kind=kOutput, calls=%fused_computation.5 | convolution fusion | flops 1650981888 | bytes 11014144 | tf_op jit(solution)/shard_map/dot_general | solution.py:72
  62.6 0.0 copy-start.1
  62.6 2.3 %fusion.12 = f32[1024]{0:T(1024)S(1)} fusion(bf16[1024,1024]{0,1:T(8,128)(2,1)} %get-tuple-element.18, f32[1024]{0:T(1024)S(1)} %broadcast_multiply_fusion.1), kind=kLoop, calls=%fused_computation.24 | loop fusion | flops 4193280 | bytes 2105344 | tf_op jit(solution)/shard_map/reduce_sum | solution.py:35
  65.0 0.0 copy-done.1
  65.0 2.8 %fusion.95 = bf16[1024,512]{1,0:T(8,128)(2,1)S(1)} fusion(bf16[1024,1024]{0,1:T(8,128)(2,1)S(1)} %copy-done.1, f32[1024]{0:T(1024)S(1)} %bitcast.97, f32[1024]{0:T(1024)S(1)} %bitcast.96, f32[1024]{0:T(1024)S(1)} %add_rsqrt_fusion.1, f32[1024]{0:T(1024)S(1)} %broadcast_multiply_fusion.1, bf16[4,1024,512]{2,1,0:T(8,128)(2,1)} %param.9), kind=kOutput, calls=%fused_computation.141 | convolution fusion | flops 1080557568 | bytes 4210688 | tf_op jit(solution)/shard_map/dot_general | solution.py:54
  67.8 1.4 collective-permute-start.4
  69.2 0.7 collective-permute-start.5
  69.9 1.7 fusion.133
  71.7 20.2 %collective-permute-done.4 = bf16[1024,512]{1,0:T(8,128)(2,1)S(1)} collective-permute-done((bf16[1024,512]{1,0:T(8,128)(2,1)S(1)}, bf16[1024,512]{1,0:T(8,128)(2,1)S(1)}, u32[]{:S(2)}, u32[]{:S(2)}) %collective-permute-start.4) | collective-permute-done | bytes 1048608 | tf_op jit(solution)/shard_map/ppermute | solution.py:15
  91.9 3.1 %fusion.131 = f32[1024,512]{1,0:T(8,128)} fusion(bf16[1024,512]{1,0:T(8,128)(2,1)S(1)} %collective-permute-done.4, bf16[4,3,512,512]{3,2,1,0:T(8,128)(2,1)} %param.10), kind=kOutput, calls=%fused_computation.171 | convolution fusion | flops 536870912 | bytes 3670016 | tf_op jit(solution)/shard_map/dot_general | solution.py:69
  94.9 1.9 %collective-permute-done.5 = bf16[1024,512]{1,0:T(8,128)(2,1)S(1)} collective-permute-done((bf16[1024,512]{1,0:T(8,128)(2,1)S(1)}, bf16[1024,512]{1,0:T(8,128)(2,1)S(1)}, u32[]{:S(2)}, u32[]{:S(2)}) %collective-permute-start.5) | collective-permute-done | bytes 1048608 | tf_op jit(solution)/shard_map/ppermute | solution.py:15
  96.8 9.8 %convert_reduce_fusion = (f32[1024]{0:T(1024)S(1)}, bf16[1024,1024]{0,1:T(8,128)(2,1)}) fusion(bf16[4,512,1024]{2,1,0:T(8,128)(2,1)} %param.11, f32[1024,512]{1,0:T(8,128)S(1)} %fusion.133, f32[1024,512]{1,0:T(8,128)} %fusion.131, bf16[1024,512]{1,0:T(8,128)(2,1)S(1)} %collective-permute-done.5, bf16[4,3,512,512]{3,2,1,0:T(8,128)(2,1)} %param.10, ...), kind=kOutput, calls=%fused_computation.2 | convolution fusion | flops 1650981888 | bytes 11014144 | tf_op jit(solution)/shard_map/dot_general | solution.py:72
  106.6 0.0 copy-start.2
  106.6 2.3 %fusion.8 = f32[1024]{0:T(1024)S(1)} fusion(bf16[1024,1024]{0,1:T(8,128)(2,1)} %get-tuple-element.20, f32[1024]{0:T(1024)S(1)} %broadcast_multiply_fusion), kind=kLoop, calls=%fused_computation.20 | loop fusion | flops 4193280 | bytes 2105344 | tf_op jit(solution)/shard_map/reduce_sum | solution.py:35
  109.0 0.0 copy-done.2
  109.0 2.8 %fusion.92 = bf16[1024,512]{1,0:T(8,128)(2,1)S(1)} fusion(bf16[1024,1024]{0,1:T(8,128)(2,1)S(1)} %copy-done.2, f32[1024]{0:T(1024)S(1)} %bitcast.95, f32[1024]{0:T(1024)S(1)} %bitcast.94, f32[1024]{0:T(1024)S(1)} %add_rsqrt_fusion, f32[1024]{0:T(1024)S(1)} %broadcast_multiply_fusion, bf16[4,1024,512]{2,1,0:T(8,128)(2,1)} %param.9), kind=kOutput, calls=%fused_computation.140 | convolution fusion | flops 1080557568 | bytes 4210688 | tf_op jit(solution)/shard_map/dot_general | solution.py:54
  111.8 4.7 %collective-permute-start.6 = (bf16[1024,512]{1,0:T(8,128)(2,1)S(1)}, bf16[1024,512]{1,0:T(8,128)(2,1)S(1)}, u32[]{:S(2)}, u32[]{:S(2)}) collective-permute-start(bf16[1024,512]{1,0:T(8,128)(2,1)S(1)} %fusion.92), channel_id=1, source_target_pairs={{0,4},{1,5},{2,6},{3,7},{4,8},{5,9},{6,10},{7,11},{8,12},{9,13},{1... | collective-permute-start | bytes 3145736 | tf_op jit(solution)/shard_map/ppermute | solution.py:15
  116.5 5.9 %collective-permute-start.7 = (bf16[1024,512]{1,0:T(8,128)(2,1)S(1)}, bf16[1024,512]{1,0:T(8,128)(2,1)S(1)}, u32[]{:S(2)}, u32[]{:S(2)}) collective-permute-start(bf16[1024,512]{1,0:T(8,128)(2,1)S(1)} %fusion.92), channel_id=1, source_target_pairs={{0,60},{1,61},{2,62},{3,63},{4,0},{5,1},{6,2},{7,3},{8,4},{9,5},{1... | collective-permute-start | bytes 3145736 | tf_op jit(solution)/shard_map/ppermute | solution.py:15
  122.4 1.7 fusion.127
  124.2 40.4 %collective-permute-done.6 = bf16[1024,512]{1,0:T(8,128)(2,1)S(1)} collective-permute-done((bf16[1024,512]{1,0:T(8,128)(2,1)S(1)}, bf16[1024,512]{1,0:T(8,128)(2,1)S(1)}, u32[]{:S(2)}, u32[]{:S(2)}) %collective-permute-start.6) | collective-permute-done | bytes 1048608 | tf_op jit(solution)/shard_map/ppermute | solution.py:15
  164.5 3.1 %fusion.125 = f32[1024,512]{1,0:T(8,128)} fusion(bf16[1024,512]{1,0:T(8,128)(2,1)S(1)} %collective-permute-done.6, bf16[4,3,512,512]{3,2,1,0:T(8,128)(2,1)} %param.10), kind=kOutput, calls=%fused_computation.166 | convolution fusion | flops 536870912 | bytes 3670016 | tf_op jit(solution)/shard_map/dot_general | solution.py:69
  167.6 0.0 collective-permute-done.7
  167.6 9.8 %fusion.27 = bf16[1024,1024]{0,1:T(8,128)(2,1)} fusion(bf16[1024,1024]{0,1:T(8,128)(2,1)} %get-tuple-element.20, bf16[4,512,1024]{2,1,0:T(8,128)(2,1)} %param.11, f32[1024,512]{1,0:T(8,128)S(1)} %fusion.127, f32[1024,512]{1,0:T(8,128)} %fusion.125, bf16[1024,512]{1,0:T(8,128)(2,1)S(1)} %collective-permute-done.7, bf16[4,3,512,512]{3,2,1,0:T(8,128)(2,1)} %param.10), kind=kOutput, calls=%fused_computation.39 | convolution fusion | flops 1648885760 | bytes 11010048 | tf_op jit(solution)/shard_map/dot_general | solution.py:72
  177.4 3.9 %copy.9 = bf16[1024,1024]{1,0:T(8,128)(2,1)} copy(bf16[1024,1024]{0,1:T(8,128)(2,1)} %fusion.27) | data formatting | bytes 4194304 | tf_op jit(solution)/shard_map/convert_element_type | solution.py:75
  (8 shorter events, 0.0 us)
Async XLA Ops:
  8.4 8.7 %collective-permute-start = (bf16[512,512]{1,0:T(8,128)(2,1)S(1)}, bf16[512,512]{1,0:T(8,128)(2,1)S(1)}, u32[]{:S(2)}, u32[]{:S(2)}) collective-permute-start(bf16[512,512]{1,0:T(8,128)(2,1)S(1)} %get-tuple-element.6), channel_id=1, source_target_pairs={{0,1},{1,2},{2,3},{3,4},{4,5},{5,6},{6,7},{7,8},{8,9},{9,10},{10,1... | collective-permute-start | bytes 1572872 | tf_op jit(solution)/shard_map/ppermute | solution.py:25
  8.5 11.6 %collective-permute-start.1 = (bf16[512,512]{1,0:T(8,128)(2,1)S(1)}, bf16[512,512]{1,0:T(8,128)(2,1)}, u32[]{:S(2)}, u32[]{:S(2)}) collective-permute-start(bf16[512,512]{1,0:T(8,128)(2,1)S(1)} %get-tuple-element.5), channel_id=1, source_target_pairs={{1,0},{2,1},{3,2},{4,3},{5,4},{6,5},{7,6},{8,7},{9,8},{10,9},{11,1... | collective-permute-start | bytes 1572872 | tf_op jit(solution)/shard_map/ppermute | solution.py:26
  30.3 2.4 %copy-start = (bf16[1024,1024]{0,1:T(8,128)(2,1)S(1)}, bf16[1024,1024]{0,1:T(8,128)(2,1)}, u32[]{:S(2)}) copy-start(bf16[1024,1024]{0,1:T(8,128)(2,1)} %get-tuple-element.16) | copy-start | bytes 6291460
  35.5 14.3 %collective-permute-start.2 = (bf16[1024,512]{1,0:T(8,128)(2,1)S(1)}, bf16[1024,512]{1,0:T(8,128)(2,1)S(1)}, u32[]{:S(2)}, u32[]{:S(2)}) collective-permute-start(bf16[1024,512]{1,0:T(8,128)(2,1)S(1)} %fusion.98), channel_id=1, source_target_pairs={{0,1},{1,2},{2,3},{3,4},{4,5},{5,6},{6,7},{7,8},{8,9},{9,10},{10,1... | collective-permute-start | bytes 3145736 | tf_op jit(solution)/shard_map/ppermute | solution.py:15
  35.6 17.3 %collective-permute-start.3 = (bf16[1024,512]{1,0:T(8,128)(2,1)S(1)}, bf16[1024,512]{1,0:T(8,128)(2,1)S(1)}, u32[]{:S(2)}, u32[]{:S(2)}) collective-permute-start(bf16[1024,512]{1,0:T(8,128)(2,1)S(1)} %fusion.98), channel_id=1, source_target_pairs={{0,63},{1,0},{2,1},{3,2},{4,3},{5,4},{6,5},{7,6},{8,7},{9,8},{10,9... | collective-permute-start | bytes 3145736 | tf_op jit(solution)/shard_map/ppermute | solution.py:15
  62.6 2.4 %copy-start.1 = (bf16[1024,1024]{0,1:T(8,128)(2,1)S(1)}, bf16[1024,1024]{0,1:T(8,128)(2,1)}, u32[]{:S(2)}) copy-start(bf16[1024,1024]{0,1:T(8,128)(2,1)} %get-tuple-element.18) | copy-start | bytes 6291460
  67.8 24.1 %collective-permute-start.4 = (bf16[1024,512]{1,0:T(8,128)(2,1)S(1)}, bf16[1024,512]{1,0:T(8,128)(2,1)S(1)}, u32[]{:S(2)}, u32[]{:S(2)}) collective-permute-start(bf16[1024,512]{1,0:T(8,128)(2,1)S(1)} %fusion.95), channel_id=1, source_target_pairs={{0,2},{1,3},{2,4},{3,5},{4,6},{5,7},{6,8},{7,9},{8,10},{9,11},{10,... | collective-permute-start | bytes 3145736 | tf_op jit(solution)/shard_map/ppermute | solution.py:15
  69.2 27.6 %collective-permute-start.5 = (bf16[1024,512]{1,0:T(8,128)(2,1)S(1)}, bf16[1024,512]{1,0:T(8,128)(2,1)S(1)}, u32[]{:S(2)}, u32[]{:S(2)}) collective-permute-start(bf16[1024,512]{1,0:T(8,128)(2,1)S(1)} %fusion.95), channel_id=1, source_target_pairs={{0,62},{1,63},{2,0},{3,1},{4,2},{5,3},{6,4},{7,5},{8,6},{9,7},{10,... | collective-permute-start | bytes 3145736 | tf_op jit(solution)/shard_map/ppermute | solution.py:15
  106.6 2.4 %copy-start.2 = (bf16[1024,1024]{0,1:T(8,128)(2,1)S(1)}, bf16[1024,1024]{0,1:T(8,128)(2,1)}, u32[]{:S(2)}) copy-start(bf16[1024,1024]{0,1:T(8,128)(2,1)} %get-tuple-element.20) | copy-start | bytes 6291460
  111.8 52.7 %collective-permute-start.6 = (bf16[1024,512]{1,0:T(8,128)(2,1)S(1)}, bf16[1024,512]{1,0:T(8,128)(2,1)S(1)}, u32[]{:S(2)}, u32[]{:S(2)}) collective-permute-start(bf16[1024,512]{1,0:T(8,128)(2,1)S(1)} %fusion.92), channel_id=1, source_target_pairs={{0,4},{1,5},{2,6},{3,7},{4,8},{5,9},{6,10},{7,11},{8,12},{9,13},{1... | collective-permute-start | bytes 3145736 | tf_op jit(solution)/shard_map/ppermute | solution.py:15
  116.5 51.1 %collective-permute-start.7 = (bf16[1024,512]{1,0:T(8,128)(2,1)S(1)}, bf16[1024,512]{1,0:T(8,128)(2,1)S(1)}, u32[]{:S(2)}, u32[]{:S(2)}) collective-permute-start(bf16[1024,512]{1,0:T(8,128)(2,1)S(1)} %fusion.92), channel_id=1, source_target_pairs={{0,60},{1,61},{2,62},{3,63},{4,0},{5,1},{6,2},{7,3},{8,4},{9,5},{1... | collective-permute-start | bytes 3145736 | tf_op jit(solution)/shard_map/ppermute | solution.py:15
where the time goes:
time: 182 us; the launch traced here: 181 us
  waiting for transfers between devices  77 us (42%)
  matrix products  71.2 us (39%)
  starting transfers between devices  16.3 us (9%)
  local copies, waits for them, and re-layouts  8.64 us (5%)
  other arithmetic  8.05 us (4%)
    ppermute x6, waiting for transfers between devices, passed_along(): lax.ppermute(array, axis, [(i, (i + by) % peers) for i in range(peers)])  73.2 us
    dot_general x4, matrix products, body(): jnp.dot(activated, output_projection[block_depth], preferred_element_type...  39.5 us
    ppermute x6, starting transfers between devices, passed_along(): lax.ppermute(array, axis, [(i, (i + by) % peers) for i in range(peers)])  14.5 us
    dot_general x4, matrix products, body(): jnp.dot(normed, proj_in[block_depth], preferred_element_type=jnp.float32)  11.2 us
    dot_general x3, matrix products, body(): jnp.dot(earlier, kernel[0], preferred_element_type=jnp.float32)  9.19 us
    dot_general x4, matrix products, body(): middle = jnp.dot(narrow, kernel[1], preferred_element_type=jnp.float32)  8.28 us
    reduce_sum x4, other arithmetic, normalize(): variance = jnp.mean(centred_values * centred_values, axis=1, keepdims=True)  7.64 us
    convert_element_type x1, local copies, waits for them, and re-layouts, body(): stream = (stream.astype(jnp.float32) + update).astype(jnp.bfloat16)  3.93 us
  transfers between devices with their start and end apart: 8, of which 5 were waited for; matrix products, arithmetic and copies ran while one was open for 11% of the time, Pallas kernels for 0%

commit v1 on v0

v1 whole, which is shorter than its diff:
```python
import functools

import jax
import jax.numpy as jnp
from jax import lax
from jax.experimental import pallas as pl
from jax.experimental.pallas import tpu as pltpu
from jax.sharding import PartitionSpec as P

MESH = pl.DeviceIdType.MESH
LAYERS = 4
UNIT = 512
EPSILON = 1e-05
GROUP = 8
SLAB = 16
BF16 = jnp.bfloat16
F32 = jnp.float32


def gelu(values):
    return 0.5 * values * (1.0 + lax.erf(values * 0.7071067811865476))


def kernel(
    peers, halves, chunks,
    x_hbm, gain_ref, bias_ref, proj_hbm, taps_hbm, outp_hbm,
    out_hbm,
    xt, narrow, proj, taps, outp,
    in_send, in_recv, own_sem, halo_send, halo_recv, out_send, out_recv, out_own, weight_sem,
):
    me = lax.axis_index("blk")
    rank = lax.rem(me, GROUP)
    base = me - rank
    above = lax.rem(me + GROUP, peers)
    below = lax.rem(me + peers - GROUP, peers)
    span = GROUP * halves
    rows = span * SLAB
    width = x_hbm.shape[-1]
    hidden = narrow.shape[-1]

    def mate(step):
        return lax.rem(rank + step, GROUP)

    def remote(src, dst, send, recv, device):
        return pltpu.make_async_remote_copy(
            src_ref=src, dst_ref=dst, send_sem=send, recv_sem=recv,
            device_id={"blk": device}, device_id_type=MESH,
        )

    def weight_copies(layer):
        return (
            pltpu.make_async_copy(proj_hbm.at[layer], proj.at[layer], weight_sem.at[layer, 0]),
            pltpu.make_async_copy(taps_hbm.at[layer], taps.at[layer], weight_sem.at[layer, 1]),
            pltpu.make_async_copy(outp_hbm.at[layer], outp.at[layer], weight_sem.at[layer, 2]),
        )

    def own_in(chunk):
        return pltpu.make_async_copy(
            x_hbm.at[:, rank, chunk], xt.at[chunk, pl.ds(halves * rank, halves)], own_sem.at[chunk]
        )

    for copy in weight_copies(0):
        copy.start()

    @pl.loop(0, chunks)
    def _(chunk):
        own_in(chunk).start()

    barrier = pltpu.get_barrier_semaphore()
    for step in range(1, GROUP):
        pl.semaphore_signal(barrier, inc=1, device_id={"blk": base + mate(step)}, device_id_type=MESH)
    for device in (above, below):
        pl.semaphore_signal(barrier, inc=1, device_id={"blk": device}, device_id_type=MESH)
    pl.semaphore_wait(barrier, GROUP + 1)

    @pl.loop(0, chunks)
    def _(chunk):
        for step in (4, 5, 3, 6, 2, 7, 1):
            to = mate(step)
            remote(
                x_hbm.at[:, to, chunk], xt.at[chunk, pl.ds(halves * rank, halves)],
                in_send.at[chunk], in_recv.at[chunk], base + to,
            ).start()

    for layer in range(1, LAYERS):
        for copy in weight_copies(layer):
            copy.start()

    def halo_copies(layer, chunk):
        reach = 2**layer
        mine = narrow.at[chunk, layer]
        up = remote(
            mine.at[pl.ds(span // 2 + span - reach, reach)], mine.at[pl.ds(span // 2 - reach, reach)],
            halo_send.at[chunk, layer, 0], halo_recv.at[chunk, layer, 0], above,
        )
        down = remote(
            mine.at[pl.ds(span // 2, reach)], mine.at[pl.ds(span // 2 + span, reach)],
            halo_send.at[chunk, layer, 1], halo_recv.at[chunk, layer, 1], below,
        )
        return up, down

    def project(layer, chunk):
        values = xt[chunk].reshape(rows, width).astype(F32)
        centred = values - jnp.mean(values, axis=1, keepdims=True)
        variance = jnp.mean(centred * centred, axis=1, keepdims=True)
        normed = centred * lax.rsqrt(variance + EPSILON) * gain_ref[pl.ds(layer, 1), :] + bias_ref[pl.ds(layer, 1), :]
        result = jnp.dot(normed.astype(BF16), proj[layer], preferred_element_type=F32).astype(BF16)
        narrow[chunk, layer, pl.ds(span // 2, span)] = result.reshape(span, SLAB, hidden)

    def update(layer, reach, chunk):
        parts = [
            narrow[chunk, layer, pl.ds(span // 2 + shift, span)].reshape(rows, hidden)
            for shift in (-reach, 0, reach)
        ]
        convolved = jnp.dot(
            jnp.concatenate(parts, axis=1), taps[layer], preferred_element_type=F32
        )
        activated = gelu(convolved).astype(BF16)
        delta = jnp.dot(activated, outp[layer], preferred_element_type=F32)
        new = (xt[chunk].reshape(rows, width).astype(F32) + delta).astype(BF16)
        xt[chunk] = new.reshape(span, SLAB, width)

    def own_out(chunk):
        return pltpu.make_async_copy(
            xt.at[chunk, pl.ds(halves * rank, halves)], out_hbm.at[:, rank, chunk], out_own.at[chunk]
        )

    def out_copies(chunk):
        return [
            remote(
                xt.at[chunk, pl.ds(halves * mate(step), halves)], out_hbm.at[:, rank, chunk],
                out_send.at[chunk], out_recv.at[chunk], base + mate(step),
            )
            for step in (4, 5, 3, 6, 2, 7, 1)
        ]

    stages = LAYERS + 1

    @pl.loop(0, stages + chunks - 1)
    def _(wave):
        @pl.loop(0, chunks)
        def _(chunk):
            stage = wave - chunk

            @pl.when(stage == 0)
            def _():
                own_in(chunk).wait()
                whole = xt.at[chunk, pl.ds(0, span - halves)]
                pltpu.make_async_copy(whole, whole, in_recv.at[chunk]).wait()

            for layer in range(LAYERS):
                @pl.when((stage == layer) & (chunk == 0))
                def _():
                    for copy in weight_copies(layer):
                        copy.wait()

                @pl.when(stage == layer + 1)
                def _():
                    for copy in halo_copies(layer, chunk):
                        copy.wait_recv()
                    update(layer, 2**layer, chunk)

                @pl.when(stage == layer)
                def _():
                    project(layer, chunk)
                    for copy in halo_copies(layer, chunk):
                        copy.start()

            @pl.when(stage == LAYERS)
            def _():
                own_out(chunk).start()
                for copy in out_copies(chunk):
                    copy.start()

    @pl.loop(0, chunks)
    def _(chunk):
        whole = xt.at[chunk, pl.ds(0, span - halves)]
        own_out(chunk).wait()
        for layer in range(LAYERS):
            for copy in halo_copies(layer, chunk):
                copy.wait_send()
        pltpu.make_async_copy(whole, whole, in_send.at[chunk]).wait()
        pltpu.make_async_copy(whole, whole, out_send.at[chunk]).wait()
        pltpu.make_async_copy(whole, whole, out_recv.at[chunk]).wait()


def solution(mesh):
    peers = mesh.shape["blk"]

    def body(stream, norm_gain, norm_bias, proj_in, convolution_taps, output_projection):
        rows, width = stream.shape
        hidden = proj_in.shape[2]
        halves = rows // UNIT
        chunks = UNIT // GROUP // SLAB
        span = GROUP * halves
        shape = (halves, GROUP, chunks, SLAB, width)
        vmem = pl.BlockSpec(memory_space=pltpu.VMEM)
        anywhere = pl.BlockSpec(memory_space=pl.ANY)
        dma = pltpu.SemaphoreType.DMA
        result = pl.pallas_call(
            functools.partial(kernel, peers, halves, chunks),
            out_shape=jax.ShapeDtypeStruct(shape, BF16),
            in_specs=[anywhere, vmem, vmem, anywhere, anywhere, anywhere],
            out_specs=anywhere,
            scratch_shapes=[
                pltpu.VMEM((chunks, span, SLAB, width), BF16),
                pltpu.VMEM((chunks, LAYERS, 2 * span, SLAB, hidden), BF16),
                pltpu.VMEM((LAYERS, width, hidden), BF16),
                pltpu.VMEM((LAYERS, 3 * hidden, hidden), BF16),
                pltpu.VMEM((LAYERS, hidden, width), BF16),
                dma((chunks,)), dma((chunks,)), dma((chunks,)),
                dma((chunks, LAYERS, 2)), dma((chunks, LAYERS, 2)),
                dma((chunks,)), dma((chunks,)), dma((chunks,)),
                dma((LAYERS, 3)),
            ],
            compiler_params=pltpu.CompilerParams(
                collective_id=0, has_side_effects=True, vmem_limit_bytes=56 * 2**20
            ),
        )(
            stream.reshape(shape), norm_gain, norm_bias, proj_in,
            convolution_taps.reshape(LAYERS, 3 * hidden, hidden), output_projection,
        )
        return result.reshape(rows, width)

    return jax.shard_map(
        body,
        mesh=mesh,
        in_specs=(P(("batch", "blk"), None), P(), P(), P(), P(), P()),
        out_specs=P(("batch", "blk"), None),
        check_vma=False,
    )
```

time: 182 us -> 73 us (0.40)
  the two profiles are of different devices: /device:TPU:16 before, /device:TPU:1 now
where the time goes in v1:
time: 73 us; the launch traced here: 72.8 us
  Pallas kernels  69.7 us (95%)
  local copies, waits for them, and re-layouts  3.08 us (4%)
    pallas_call x1, Pallas kernels, body(): pl.pallas_call(functools.partial(kernel, peers, halves, chunks), out_shap...  69.7 us
    unnamed x1, local copies, waits for them, and re-layouts  3.08 us

profile of v1, /device:TPU:1, one launch (start us, length us, event | category | flops | bytes accessed | tf_op | source)
XLA Modules:
  0.0 72.8 jit_solution(10476143330535767431)
XLA Ops:
  0.0 69.7 %shard_map.64 = bf16[2,8,4,16,1024]{4,3,2,1,0:T(8,128)(2,1)} custom-call(bf16[2,8,4,16,1024]{4,3,2,1,0:T(8,128)(2,1)} %bitcast.5, f32[4,1024]{1,0:T(4,128)} %gain_ref.1, f32[4,1024]{1,0:T(4,128)} %bias_ref.1, bf16[4,1024,512]{2,1,0:T(8,128)(2,1)} %proj_hbm.1, bf16[4,1536,512]{2,1,0:T(8,128)(2,1)} %bitcast.4, bf16[4,512,1024]{2,1,0:T(8,128)(2,1)} %outp_hbm.1), custom_call_target="tpu_custom_call" | custom-call | tf_op jit(solution)/shard_map/pallas_call | solution.py:200
  69.7 3.1 %copy.8 = bf16[1024,1024]{1,0:T(8,128)(2,1)} copy(bf16[1024,1024]{1,0:T(8,128)(2,1)} %bitcast.3) | data formatting | bytes 4194304

commit v2 on v1

--- a/solution.py
+++ b/solution.py
@@ -13,6 +13,9 @@
 EPSILON = 1e-05
 GROUP = 8
 SLAB = 16
+ORDER = ((2, 0), (2, 1), (1, 0), (3, 0), (1, 1), (3, 1), (0, 1))
+AHEAD = 4
+SCHEDULE = (0, 10, 1, 20, 11, 2, 30, 21, 12, 3, 40, 31, 22, 13, 41, 32, 23, 42, 33, 43)
 BF16 = jnp.bfloat16
 F32 = jnp.float32
 
@@ -24,7 +27,7 @@
 def kernel(
     peers, halves, chunks,
     x_hbm, gain_ref, bias_ref, proj_hbm, taps_hbm, outp_hbm,
-    out_hbm,
+    out_ref,
     xt, narrow, proj, taps, outp,
     in_send, in_recv, own_sem, halo_send, halo_recv, out_send, out_recv, out_own, weight_sem,
 ):
@@ -38,8 +41,8 @@
     width = x_hbm.shape[-1]
     hidden = narrow.shape[-1]
 
-    def mate(step):
-        return lax.rem(rank + step, GROUP)
+    def mate(chip, core):
+        return lax.rem(rank + 2 * chip - lax.rem(rank, 2), GROUP) + lax.rem(rank + core, 2)
 
     def remote(src, dst, send, recv, device):
         return pltpu.make_async_remote_copy(
@@ -67,20 +70,23 @@
         own_in(chunk).start()
 
     barrier = pltpu.get_barrier_semaphore()
-    for step in range(1, GROUP):
-        pl.semaphore_signal(barrier, inc=1, device_id={"blk": base + mate(step)}, device_id_type=MESH)
+    for step in ORDER:
+        pl.semaphore_signal(barrier, inc=1, device_id={"blk": base + mate(*step)}, device_id_type=MESH)
     for device in (above, below):
         pl.semaphore_signal(barrier, inc=1, device_id={"blk": device}, device_id_type=MESH)
     pl.semaphore_wait(barrier, GROUP + 1)
 
-    @pl.loop(0, chunks)
-    def _(chunk):
-        for step in (4, 5, 3, 6, 2, 7, 1):
-            to = mate(step)
+    def send_in(chunk):
+        for step in ORDER:
+            to = mate(*step)
             remote(
                 x_hbm.at[:, to, chunk], xt.at[chunk, pl.ds(halves * rank, halves)],
                 in_send.at[chunk], in_recv.at[chunk], base + to,
             ).start()
+
+    @pl.loop(0, AHEAD)
+    def _(chunk):
+        send_in(chunk)
 
     for layer in range(1, LAYERS):
         for copy in weight_copies(layer):
@@ -99,15 +105,18 @@
         )
         return up, down
 
-    def project(layer, chunk):
-        values = xt[chunk].reshape(rows, width).astype(F32)
+    def stream_of(chunk):
+        return xt[chunk].reshape(rows, width).astype(F32)
+
+    def project(values, layer, chunk):
         centred = values - jnp.mean(values, axis=1, keepdims=True)
         variance = jnp.mean(centred * centred, axis=1, keepdims=True)
         normed = centred * lax.rsqrt(variance + EPSILON) * gain_ref[pl.ds(layer, 1), :] + bias_ref[pl.ds(layer, 1), :]
         result = jnp.dot(normed.astype(BF16), proj[layer], preferred_element_type=F32).astype(BF16)
         narrow[chunk, layer, pl.ds(span // 2, span)] = result.reshape(span, SLAB, hidden)
 
-    def update(layer, reach, chunk):
+    def update(layer, chunk):
+        reach = jnp.where(layer == 0, 1, jnp.where(layer == 1, 2, jnp.where(layer == 2, 4, 8)))
         parts = [
             narrow[chunk, layer, pl.ds(span // 2 + shift, span)].reshape(rows, hidden)
             for shift in (-reach, 0, reach)
@@ -117,60 +126,83 @@
         )
         activated = gelu(convolved).astype(BF16)
         delta = jnp.dot(activated, outp[layer], preferred_element_type=F32)
-        new = (xt[chunk].reshape(rows, width).astype(F32) + delta).astype(BF16)
+        new = (stream_of(chunk) + delta).astype(BF16)
         xt[chunk] = new.reshape(span, SLAB, width)
+        return new.astype(F32)
 
     def own_out(chunk):
         return pltpu.make_async_copy(
-            xt.at[chunk, pl.ds(halves * rank, halves)], out_hbm.at[:, rank, chunk], out_own.at[chunk]
+            xt.at[chunk, pl.ds(halves * rank, halves)], out_ref.at[:, rank, chunk], out_own.at[chunk]
         )
 
     def out_copies(chunk):
         return [
             remote(
-                xt.at[chunk, pl.ds(halves * mate(step), halves)], out_hbm.at[:, rank, chunk],
-                out_send.at[chunk], out_recv.at[chunk], base + mate(step),
+                xt.at[chunk, pl.ds(halves * mate(*step), halves)], out_ref.at[:, rank, chunk],
+                out_send.at[chunk], out_recv.at[chunk], base + mate(*step),
             )
-            for step in (4, 5, 3, 6, 2, 7, 1)
+            for step in ORDER
         ]
 
-    stages = LAYERS + 1
-
-    @pl.loop(0, stages + chunks - 1)
-    def _(wave):
-        @pl.loop(0, chunks)
-        def _(chunk):
-            stage = wave - chunk
-
-            @pl.when(stage == 0)
-            def _():
-                own_in(chunk).wait()
-                whole = xt.at[chunk, pl.ds(0, span - halves)]
-                pltpu.make_async_copy(whole, whole, in_recv.at[chunk]).wait()
-
-            for layer in range(LAYERS):
-                @pl.when((stage == layer) & (chunk == 0))
-                def _():
-                    for copy in weight_copies(layer):
-                        copy.wait()
-
-                @pl.when(stage == layer + 1)
-                def _():
-                    for copy in halo_copies(layer, chunk):
-                        copy.wait_recv()
-                    update(layer, 2**layer, chunk)
-
-                @pl.when(stage == layer)
-                def _():
-                    project(layer, chunk)
-                    for copy in halo_copies(layer, chunk):
-                        copy.start()
-
-            @pl.when(stage == LAYERS)
-            def _():
-                own_out(chunk).start()
-                for copy in out_copies(chunk):
+    def step(stage, chunk):
+        @pl.when(stage == 0)
+        def _():
+            own_in(chunk).wait()
+            whole = xt.at[chunk, pl.ds(0, span - halves)]
+            pltpu.make_async_copy(whole, whole, in_recv.at[chunk]).wait()
+
+            @pl.when(chunk + AHEAD < chunks)
+            def _():
+                send_in(chunk + AHEAD)
+
+        for layer in range(LAYERS):
+            @pl.when((stage == layer) & (chunk == 0))
+            def _():
+                for copy in weight_copies(layer):
+                    copy.wait()
+
+            @pl.when(stage == layer + 1)
+            def _():
+                for copy in halo_copies(layer, chunk):
+                    copy.wait_recv()
+
+        @pl.when(stage == 0)
+        def _():
+            project(stream_of(chunk), 0, chunk)
+
+        @pl.when((stage > 0) & (stage < LAYERS))
+        def _():
+            project(update(stage - 1, chunk), stage, chunk)
+
+        @pl.when(stage == LAYERS)
+        def _():
+            update(LAYERS - 1, chunk)
+
+        for layer in range(LAYERS):
+            @pl.when(stage == layer)
+            def _():
+                for copy in halo_copies(layer, chunk):
                     copy.start()
+
+        @pl.when(stage == LAYERS)
+        def _():
+            own_out(chunk).start()
+            for copy in out_copies(chunk):
+                copy.start()
+
+    order = [divmod(item, 10) for item in SCHEDULE]
+    words = [
+        sum((stage * 4 + chunk) << 5 * i for i, (stage, chunk) in enumerate(order[at : at + 6]))
+        for at in range(0, len(order), 6)
+    ]
+
+    def advance(_, codes):
+        item = codes[0] & 31
+        step(item >> 2, item & 3)
+        rest = [(codes[i] >> 5) + ((codes[i + 1] & 31) << 25) for i in range(len(codes) - 1)]
+        return (*rest, codes[-1] >> 5)
+
+    lax.fori_loop(0, len(order), advance, tuple(jnp.int32(word) for word in words))
 
     @pl.loop(0, chunks)
     def _(chunk):
@@ -199,9 +231,9 @@
         dma = pltpu.SemaphoreType.DMA
         result = pl.pallas_call(
             functools.partial(kernel, peers, halves, chunks),
-            out_shape=jax.ShapeDtypeStruct(shape, BF16),
+            out_shape=pltpu.VMEM(shape, BF16),
             in_specs=[anywhere, vmem, vmem, anywhere, anywhere, anywhere],
-            out_specs=anywhere,
+            out_specs=vmem,
             scratch_shapes=[
                 pltpu.VMEM((chunks, span, SLAB, width), BF16),
                 pltpu.VMEM((chunks, LAYERS, 2 * span, SLAB, hidden), BF16),

time: 73 us -> 71.9 us (0.985)
  local copies, waits for them, and re-layouts: 3.08 us -> 1.32 us
    unnamed x1, local copies, waits for them, and re-layouts: 3.08 us -> 1.32 us
where the time goes in v2:
time: 71.9 us; the launch traced here: 71.6 us
  Pallas kernels  70.3 us (98%)
  local copies, waits for them, and re-layouts  1.32 us (2%)
    pallas_call x1, Pallas kernels, body(): pl.pallas_call(functools.partial(kernel, peers, halves, chunks), out_shap...  70.3 us

profile of v2, /device:TPU:1, one launch (start us, length us, event | category | flops | bytes accessed | tf_op | source)
XLA Modules:
  0.0 71.6 jit_solution(10513425409396467053)
XLA Ops:
  0.0 70.3 %shard_map.64 = bf16[2,8,4,16,1024]{4,3,2,1,0:T(8,128)(2,1)S(1)} custom-call(bf16[2,8,4,16,1024]{4,3,2,1,0:T(8,128)(2,1)} %bitcast.5, f32[4,1024]{1,0:T(4,128)} %gain_ref.1, f32[4,1024]{1,0:T(4,128)} %bias_ref.1, bf16[4,1024,512]{2,1,0:T(8,128)(2,1)} %proj_hbm.1, bf16[4,1536,512]{2,1,0:T(8,128)(2,1)} %bitcast.4, bf16[4,512,1024]{2,1,0:T(8,128)(2,1)} %outp_hbm.1), custom_call_target="tpu_custom_call" | custom-call | tf_op jit(solution)/shard_map/pallas_call | solution.py:232
  70.3 1.3 %copy.8 = bf16[1024,1024]{1,0:T(8,128)(2,1)} copy(bf16[1024,1024]{1,0:T(8,128)(2,1)S(1)} %bitcast.3) | data formatting | bytes 4194304

commit v3 on v1

--- a/solution.py
+++ b/solution.py
@@ -24,7 +24,7 @@
 def kernel(
     peers, halves, chunks,
     x_hbm, gain_ref, bias_ref, proj_hbm, taps_hbm, outp_hbm,
-    out_hbm,
+    out_ref,
     xt, narrow, proj, taps, outp,
     in_send, in_recv, own_sem, halo_send, halo_recv, out_send, out_recv, out_own, weight_sem,
 ):
@@ -99,36 +99,43 @@
         )
         return up, down
 
-    def project(layer, chunk):
-        values = xt[chunk].reshape(rows, width).astype(F32)
+    def stream_of(chunk):
+        return xt[chunk].reshape(rows, width).astype(F32)
+
+    def project(values, layer, chunk):
         centred = values - jnp.mean(values, axis=1, keepdims=True)
         variance = jnp.mean(centred * centred, axis=1, keepdims=True)
         normed = centred * lax.rsqrt(variance + EPSILON) * gain_ref[pl.ds(layer, 1), :] + bias_ref[pl.ds(layer, 1), :]
         result = jnp.dot(normed.astype(BF16), proj[layer], preferred_element_type=F32).astype(BF16)
         narrow[chunk, layer, pl.ds(span // 2, span)] = result.reshape(span, SLAB, hidden)
 
-    def update(layer, reach, chunk):
-        parts = [
-            narrow[chunk, layer, pl.ds(span // 2 + shift, span)].reshape(rows, hidden)
-            for shift in (-reach, 0, reach)
-        ]
-        convolved = jnp.dot(
-            jnp.concatenate(parts, axis=1), taps[layer], preferred_element_type=F32
-        )
+    def rows_at(layer, chunk, shift):
+        return narrow[chunk, layer, pl.ds(span // 2 + shift, span)].reshape(rows, hidden)
+
+    def update(layer, chunk):
+        reach = 2**layer
+        halos = halo_copies(layer, chunk)
+        middle = jnp.dot(rows_at(layer, chunk, 0), taps[layer, pl.ds(hidden, hidden)], preferred_element_type=F32)
+        for copy in halos:
+            copy.wait_recv()
+        before = jnp.dot(rows_at(layer, chunk, -reach), taps[layer, pl.ds(0, hidden)], preferred_element_type=F32)
+        after = jnp.dot(rows_at(layer, chunk, reach), taps[layer, pl.ds(2 * hidden, hidden)], preferred_element_type=F32)
+        convolved = before + middle + after
         activated = gelu(convolved).astype(BF16)
         delta = jnp.dot(activated, outp[layer], preferred_element_type=F32)
-        new = (xt[chunk].reshape(rows, width).astype(F32) + delta).astype(BF16)
+        new = (stream_of(chunk) + delta).astype(BF16)
         xt[chunk] = new.reshape(span, SLAB, width)
+        return new.astype(F32)
 
     def own_out(chunk):
         return pltpu.make_async_copy(
-            xt.at[chunk, pl.ds(halves * rank, halves)], out_hbm.at[:, rank, chunk], out_own.at[chunk]
+            xt.at[chunk, pl.ds(halves * rank, halves)], out_ref.at[:, rank, chunk], out_own.at[chunk]
         )
 
     def out_copies(chunk):
         return [
             remote(
-                xt.at[chunk, pl.ds(halves * mate(step), halves)], out_hbm.at[:, rank, chunk],
+                xt.at[chunk, pl.ds(halves * mate(step), halves)], out_ref.at[:, rank, chunk],
                 out_send.at[chunk], out_recv.at[chunk], base + mate(step),
             )
             for step in (4, 5, 3, 6, 2, 7, 1)
@@ -148,23 +155,31 @@
                 whole = xt.at[chunk, pl.ds(0, span - halves)]
                 pltpu.make_async_copy(whole, whole, in_recv.at[chunk]).wait()
 
-            for layer in range(LAYERS):
+            @pl.when((stage == 0) & (chunk == 0))
+            def _():
+                for copy in weight_copies(0):
+                    copy.wait()
+
+            @pl.when(stage == 0)
+            def _():
+                project(stream_of(chunk), 0, chunk)
+                for copy in halo_copies(0, chunk):
+                    copy.start()
+
+            for layer in range(1, LAYERS):
                 @pl.when((stage == layer) & (chunk == 0))
                 def _():
                     for copy in weight_copies(layer):
                         copy.wait()
 
+            for layer in range(LAYERS):
                 @pl.when(stage == layer + 1)
                 def _():
-                    for copy in halo_copies(layer, chunk):
-                        copy.wait_recv()
-                    update(layer, 2**layer, chunk)
-
-                @pl.when(stage == layer)
-                def _():
-                    project(layer, chunk)
-                    for copy in halo_copies(layer, chunk):
-                        copy.start()
+                    new = update(layer, chunk)
+                    if layer + 1 < LAYERS:
+                        project(new, layer + 1, chunk)
+                        for copy in halo_copies(layer + 1, chunk):
+                            copy.start()
 
             @pl.when(stage == LAYERS)
             def _():
@@ -199,9 +214,9 @@
         dma = pltpu.SemaphoreType.DMA
         result = pl.pallas_call(
             functools.partial(kernel, peers, halves, chunks),
-            out_shape=jax.ShapeDtypeStruct(shape, BF16),
+            out_shape=pltpu.VMEM(shape, BF16),
             in_specs=[anywhere, vmem, vmem, anywhere, anywhere, anywhere],
-            out_specs=anywhere,
+            out_specs=vmem,
             scratch_shapes=[
                 pltpu.VMEM((chunks, span, SLAB, width), BF16),
                 pltpu.VMEM((chunks, LAYERS, 2 * span, SLAB, hidden), BF16),

time: 73 us -> 70.5 us (0.966)
  local copies, waits for them, and re-layouts: 3.08 us -> 1.32 us
    unnamed x1, local copies, waits for them, and re-layouts: 3.08 us -> 1.32 us
where the time goes in v3:
time: 70.5 us; the launch traced here: 70.3 us
  Pallas kernels  69 us (98%)
  local copies, waits for them, and re-layouts  1.32 us (2%)
    pallas_call x1, Pallas kernels, body(): pl.pallas_call(functools.partial(kernel, peers, halves, chunks), out_shap...  69 us

profile of v3, /device:TPU:1, one launch (start us, length us, event | category | flops | bytes accessed | tf_op | source)
XLA Modules:
  0.0 70.3 jit_solution(11426149329190677347)
XLA Ops:
  0.0 69.0 %shard_map.64 = bf16[2,8,4,16,1024]{4,3,2,1,0:T(8,128)(2,1)S(1)} custom-call(bf16[2,8,4,16,1024]{4,3,2,1,0:T(8,128)(2,1)} %bitcast.5, f32[4,1024]{1,0:T(4,128)} %gain_ref.1, f32[4,1024]{1,0:T(4,128)} %bias_ref.1, bf16[4,1024,512]{2,1,0:T(8,128)(2,1)} %proj_hbm.1, bf16[4,1536,512]{2,1,0:T(8,128)(2,1)} %bitcast.4, bf16[4,512,1024]{2,1,0:T(8,128)(2,1)} %outp_hbm.1), custom_call_target="tpu_custom_call" | custom-call | tf_op jit(solution)/shard_map/pallas_call | solution.py:215
  69.0 1.3 %copy.8 = bf16[1024,1024]{1,0:T(8,128)(2,1)} copy(bf16[1024,1024]{1,0:T(8,128)(2,1)S(1)} %bitcast.3) | data formatting | bytes 4194304

commit v4 on v3

--- a/solution.py
+++ b/solution.py
@@ -59,18 +59,19 @@
             x_hbm.at[:, rank, chunk], xt.at[chunk, pl.ds(halves * rank, halves)], own_sem.at[chunk]
         )
 
-    for copy in weight_copies(0):
-        copy.start()
-
-    @pl.loop(0, chunks)
-    def _(chunk):
-        own_in(chunk).start()
-
     barrier = pltpu.get_barrier_semaphore()
     for step in range(1, GROUP):
         pl.semaphore_signal(barrier, inc=1, device_id={"blk": base + mate(step)}, device_id_type=MESH)
     for device in (above, below):
         pl.semaphore_signal(barrier, inc=1, device_id={"blk": device}, device_id_type=MESH)
+
+    for copy in weight_copies(0):
+        copy.start()
+
+    @pl.loop(0, chunks)
+    def _(chunk):
+        own_in(chunk).start()
+
     pl.semaphore_wait(barrier, GROUP + 1)
 
     @pl.loop(0, chunks)

time: 70.5 us -> 70.5 us (level)
  no operation moved by 1% of the time
where the time goes in v4:
time: 70.5 us; the launch traced here: 70.3 us
  Pallas kernels  69 us (98%)
  local copies, waits for them, and re-layouts  1.32 us (2%)
    pallas_call x1, Pallas kernels, body(): pl.pallas_call(functools.partial(kernel, peers, halves, chunks), out_shap...  69 us

profile of v4, /device:TPU:1, one launch (start us, length us, event | category | flops | bytes accessed | tf_op | source)
XLA Modules:
  0.0 70.3 jit_solution(4396310265282310937)
XLA Ops:
  0.0 69.0 %shard_map.64 = bf16[2,8,4,16,1024]{4,3,2,1,0:T(8,128)(2,1)S(1)} custom-call(bf16[2,8,4,16,1024]{4,3,2,1,0:T(8,128)(2,1)} %bitcast.5, f32[4,1024]{1,0:T(4,128)} %gain_ref.1, f32[4,1024]{1,0:T(4,128)} %bias_ref.1, bf16[4,1024,512]{2,1,0:T(8,128)(2,1)} %proj_hbm.1, bf16[4,1536,512]{2,1,0:T(8,128)(2,1)} %bitcast.4, bf16[4,512,1024]{2,1,0:T(8,128)(2,1)} %outp_hbm.1), custom_call_target="tpu_custom_call" | custom-call | tf_op jit(solution)/shard_map/pallas_call | solution.py:216
  69.0 1.3 %copy.8 = bf16[1024,1024]{1,0:T(8,128)(2,1)} copy(bf16[1024,1024]{1,0:T(8,128)(2,1)S(1)} %bitcast.3) | data formatting | bytes 4194304
